TPU v7x, 512 devices: a whole 4x4x16 slice. The times are simulated.
512 devices in a mesh: lat: 4 (over y_hi, core), lon: 128 (over x, z, y_lo).
Axes of the slice: x: 4, y: 4 (y_hi: 2, y_lo: 2; y = y_hi * 2 + y_lo), z: 16, core: 2. Of those that a mesh axis runs over, the one named last changes fastest.
Arguments:
- features: bfloat16 [128, 1024, 1024], P('lat', 'lon'), may hold values from -18 to 18
- depth_kernel: bfloat16 [7, 7, 1024], replicated, may hold values from -0.875 to 0.875
- depth_bias: float32 [1024], replicated, may hold values from -3 to 3
- norm_gain: float32 [1024], replicated, may hold values from 0.1 to 1.9
- norm_bias: float32 [1024], replicated, may hold values from -3 to 3
- up_weight: bfloat16 [1024, 4096], P('lon', 'lat'), may hold values from -0.1875 to 0.1875
- up_bias: float32 [4096], P('lat'), may hold values from -3 to 3
- down_weight: bfloat16 [1024, 4096], P('lon', 'lat'), may hold values from -0.09375 to 0.09375
- down_bias: float32 [1024], replicated, may hold values from -3 to 3
- layer_scale: float32 [1024], replicated, may hold values from 0.3 to 2
Outputs:
- updated: bfloat16 [128, 1024, 1024], P('lat', 'lon')
All inputs are finite; a program needn't handle non-finite values.
Results may differ from a plain program's by a relative error of at most 0.0085.
Values may be sent and summed in bfloat16 or wider, within the bound.
A program may use at most 64 MiB of HBM per device.

v0:
```python
import jax
import jax.numpy as jnp
from jax import lax
from jax.sharding import PartitionSpec as P


def with_halo(block, sides, width, periodic):
    for axis, dim in sides:
        count = lax.axis_size(axis)
        forward = [(i, i + 1) for i in range(count - 1)]
        if periodic:
            forward.append((count - 1, 0))
        backward = [(target, source) for source, target in forward]
        low = lax.ppermute(
            lax.slice_in_dim(block, block.shape[dim] - width, None, axis=dim), axis, forward
        )
        high = lax.ppermute(lax.slice_in_dim(block, 0, width, axis=dim), axis, backward)
        block = jnp.concatenate([low, block, high], axis=dim)
    return block


def local(
    features,
    depth_kernel,
    depth_bias,
    norm_gain,
    norm_bias,
    up_weight,
    up_bias,
    down_weight,
    down_bias,
    layer_scale,
):
    row_count, col_count, chan_count = features.shape
    circled = with_halo(features, (("lon", 1),), 3, True)
    padded = with_halo(circled, (("lat", 0),), 3, False)
    kernel = depth_kernel.astype(jnp.float32)
    total = jnp.zeros((row_count, col_count, chan_count), jnp.float32) + depth_bias
    for row_off in range(7):
        for col_off in range(7):
            window = padded[row_off : row_off + row_count, col_off : col_off + col_count].astype(
                jnp.float32
            )
            total = total + window * kernel[row_off, col_off]
    centre = jnp.mean(total, axis=-1, keepdims=True)
    spread = jnp.mean((total - centre) ** 2, axis=-1, keepdims=True)
    normed = ((total - centre) * lax.rsqrt(spread + 1e-06) * norm_gain + norm_bias).astype(
        jnp.bfloat16
    )
    normed = normed.reshape(row_count * col_count, chan_count)
    gathered = lax.all_gather(normed, "lat", axis=0, tiled=True)
    pre = (
        jnp.dot(
            gathered,
            lax.all_gather(up_weight, "lon", axis=0, tiled=True),
            preferred_element_type=jnp.float32,
        )
        + up_bias
    )
    hidden = jax.nn.gelu(pre, approximate=False).astype(jnp.bfloat16)
    partial_out = lax.dot_general(
        hidden,
        lax.all_gather(down_weight, "lon", axis=0, tiled=True),
        (((1,), (1,)), ((), ())),
        preferred_element_type=jnp.float32,
    )
    branch = lax.psum_scatter(
        partial_out.astype(jnp.bfloat16), "lat", scatter_dimension=0, tiled=True
    ).astype(jnp.float32)
    branch = branch.reshape(row_count, col_count, chan_count)
    updated = features.astype(jnp.float32) + layer_scale * (branch + down_bias)
    return updated.astype(jnp.bfloat16)


def solution(mesh):
    placed = (
        P("lat", "lon", None),
        P(),
        P(),
        P(),
        P(),
        P("lon", "lat"),
        P("lat"),
        P("lon", "lat"),
        P(),
        P(),
    )
    return jax.shard_map(
        local, mesh=mesh, in_specs=placed, out_specs=P("lat", "lon", None), check_vma=False
    )
```

profile of v0, /device:TPU:1, one launch (start us, length us, event | category | flops | bytes accessed | tf_op | source)
XLA Modules:
  0.0 1329.8 jit_solution(5070489163931986096)
XLA Ops:
  6.5 0.0 copy-start
  6.5 0.0 all-gather.4.cloned.1.call-start
  6.5 1.5 fusion.79
  8.0 4.0 collective-permute-start
  12.0 13.0 collective-permute-start.1
  25.1 1.1 fusion.80
  26.3 1.2 fusion.81
  27.5 1.1 constant_dynamic-update-slice_fusion.1
  28.6 1.1 fusion.82
  29.7 0.0 collective-permute-done
  29.7 0.4 collective-permute-done.1
  30.1 0.0 copy-done
  30.1 0.1 pad_maximum_fusion.4
  30.2 6.0 collective-permute-start.2
  36.1 0.0 copy-start.1
  36.1 1.9 collective-permute-start.3
  38.1 0.2 constant_dynamic-update-slice_fusion
  38.3 0.0 collective-permute-done.2
  38.3 5.3 collective-permute-done.3
  43.6 0.7 maximum_maximum_fusion
  44.2 0.0 copy-done.1
  44.3 0.0 copy-start.2
  44.3 0.0 copy-start.3
  44.3 9.4 fusion.77
  53.7 0.0 copy-start.6
  53.7 0.3 multiply_reduce_fusion
  54.0 0.0 copy-done.2
  54.0 0.0 copy-done.3
  54.0 1.0 fusion.44
  55.1 0.0 all-gather.4.cloned.1.call-update
  55.1 0.0 all-gather.6.cloned.1.call-start
  55.1 0.7 all-gather.6.cloned.1.call-update
  55.8 0.0 all-gather.8.cloned.1.call-start
  55.9 0.7 all-gather.8.cloned.1.call-update
  56.6 0.0 reduce-scatter.2.cloned.1.call-start
  56.6 30.5 %all-gather.4.cloned.1.call-done = bf16[1024,1024]{1,0:T(8,128)(2,1)} async-done(((bf16[256,1024]{1,0:T(8,128)(2,1)}), bf16[1024,1024]{1,0:T(8,128)(2,1)}) %all-gather.4.cloned.1.call-update) | async-done | bytes 2097168 | tf_op jit(solution)/shard_map/all_gather | solution.py:51
  87.2 503.7 %all-gather.6.cloned.1.call-done = bf16[1024,1024]{1,0:T(8,128)(2,1)} async-done(((bf16[8,1024]{1,0:T(8,128)(2,1)}), bf16[1024,1024]{1,0:T(8,128)(2,1)}) %all-gather.6.cloned.1.call-update) | async-done | bytes 2097168 | tf_op jit(solution)/shard_map/all_gather | solution.py:55
  590.9 582.4 %all-gather.8.cloned.1.call-done = bf16[1024,1024]{1,0:T(8,128)(2,1)} async-done(((bf16[8,1024]{1,0:T(8,128)(2,1)}), bf16[1024,1024]{1,0:T(8,128)(2,1)}) %all-gather.8.cloned.1.call-update) | async-done | bytes 2097168 | tf_op jit(solution)/shard_map/all_gather | solution.py:63
  1173.3 0.0 copy-done.6
  1173.3 16.1 %fusion.14 = bf16[1024,1024]{1,0:T(8,128)(2,1)} fusion(bf16[1024,1024]{1,0:T(8,128)(2,1)} %all-gather.8.cloned.1.call-done, f32[1024]{0:T(1024)S(1)} %copy-done.6, bf16[1024,1024]{1,0:T(8,128)(2,1)} %all-gather.4.cloned.1.call-done, bf16[1024,1024]{1,0:T(8,128)(2,1)} %all-gather.6.cloned.1.call-done), kind=kOutput, calls=%fused_computation.21 | convolution fusion | flops 4365221888 | bytes 8392704 | tf_op jit(solution)/shard_map/dot_general | solution.py:61
  1189.4 0.0 copy-start.4
  1189.4 0.0 copy-start.5
  1189.4 0.0 reduce-scatter.2.cloned.1.call-update
  1189.5 131.8 %reduce-scatter.2.cloned.1.call-done = bf16[256,1024]{1,0:T(8,128)(2,1)} async-done(((bf16[1024,1024]{1,0:T(8,128)(2,1)}), bf16[256,1024]{1,0:T(8,128)(2,1)}) %reduce-scatter.2.cloned.1.call-update) | async-done | bytes 524304 | tf_op jit(solution)/shard_map/reduce_scatter | solution.py:67
  1321.2 0.0 copy-done.4
  1321.2 0.0 copy-done.5
  1321.2 2.0 fusion.42
  (2 shorter events, 0.0 us)
Async XLA Ops:
  6.5 23.5 %copy-start = (bf16[32,8,1024]{2,1,0:T(8,128)(2,1)S(1)}, bf16[32,8,1024]{2,1,0:T(8,128)(2,1)}, u32[]{:S(2)}) copy-start(bf16[32,8,1024]{2,1,0:T(8,128)(2,1)} %param.10) | copy-start | bytes 1572868
  6.5 80.6 %all-gather.4.cloned.1.call-start = ((), (), s32[]{:S(2)}) async-start(), calls=%async_computation.1 | async-start | bytes 2621440 | tf_op jit(solution)/shard_map/all_gather | solution.py:51
  8.0 21.7 %collective-permute-start = (bf16[32,3,1024]{2,1,0:T(4,128)(2,1)S(1)}, bf16[32,3,1024]{2,1,0:T(4,128)(2,1)S(1)}, u32[]{:S(2)}, u32[]{:S(2)}) collective-permute-start(bf16[32,3,1024]{2,1,0:T(4,128)(2,1)S(1)} %get-tuple-element.11), channel_id=1, source_target_pairs={{0,1},{1,2},{2,3},{3,4},{4,5},{5,6},{6,7},{7,8},{8,9},{9,10},{10,1... | collective-permute-start | bytes 589832 | tf_op jit(solution)/shard_map/ppermute | solution.py:14
  12.0 18.0 %collective-permute-start.1 = (bf16[32,3,1024]{2,1,0:T(4,128)(2,1)S(1)}, bf16[32,3,1024]{2,1,0:T(4,128)(2,1)S(1)}, u32[]{:S(2)}, u32[]{:S(2)}) collective-permute-start(bf16[32,3,1024]{2,1,0:T(4,128)(2,1)S(1)} %get-tuple-element.12), channel_id=1, source_target_pairs={{1,0},{2,1},{3,2},{4,3},{5,4},{6,5},{7,6},{8,7},{9,8},{10,9},{11,1... | collective-permute-start | bytes 589832 | tf_op jit(solution)/shard_map/ppermute | solution.py:17
  30.2 8.1 collective-permute-start.2
  36.1 8.1 copy-start.1
  36.1 7.4 collective-permute-start.3
  44.3 9.7 copy-start.2
  44.3 9.7 copy-start.3
  53.7 1119.6 %copy-start.6 = (f32[1024]{0:T(1024)S(1)}, f32[1024]{0:T(1024)}, u32[]{:S(2)}) copy-start(f32[1024]{0:T(1024)} %param.16) | copy-start | bytes 12292
  55.1 535.8 %all-gather.6.cloned.1.call-start = ((), (), s32[]{:S(2)}) async-start(), calls=%async_computation.2 | async-start | bytes 2113536 | tf_op jit(solution)/shard_map/all_gather | solution.py:55
  55.8 1117.5 %all-gather.8.cloned.1.call-start = ((), (), s32[]{:S(2)}) async-start(), calls=%async_computation.3 | async-start | bytes 2113536 | tf_op jit(solution)/shard_map/all_gather | solution.py:63
  56.6 1264.7 %reduce-scatter.2.cloned.1.call-start = ((), (), s32[]{:S(2)}) async-start(), calls=%async_computation.4 | async-start | bytes 2621440 | tf_op jit(solution)/shard_map/reduce_scatter | solution.py:67
  1189.4 131.8 %copy-start.4 = (f32[1024]{0:T(1024)S(1)}, f32[1024]{0:T(1024)}, u32[]{:S(2)}) copy-start(f32[1024]{0:T(1024)} %param.18) | copy-start | bytes 12292
  1189.4 131.8 %copy-start.5 = (f32[1024]{0:T(1024)S(1)}, f32[1024]{0:T(1024)}, u32[]{:S(2)}) copy-start(f32[1024]{0:T(1024)} %param.19) | copy-start | bytes 12292
Sparse Core Ops, SparseCore 0:
  55.2 31.9 all-gather.3
  89.2 501.5 all-gather.5
  592.9 580.2 all-gather.7
  1189.6 131.5 reduce-scatter.1
where the time goes:
time: 1330 us
  waiting for transfers between devices  1260 us (95%)
  starting transfers between devices  25.1 us (2%)
  matrix products  16.1 us (1%)
  other arithmetic  13.5 us (1%)
  between operations  13.3 us (1%)
    all_gather x1, waiting for transfers between devices, local(): lax.all_gather(down_weight, 'lon', axis=0, tiled=True)  582 us
    all_gather x1, waiting for transfers between devices, local(): lax.all_gather(up_weight, 'lon', axis=0, tiled=True)  504 us
    reduce_scatter x1, waiting for transfers between devices, local(): lax.psum_scatter(partial_out.astype(jnp.bfloat16), 'lat', scatter_dimensi...  132 us
    all_gather x1, waiting for transfers between devices, local(): gathered = lax.all_gather(normed, 'lat', axis=0, tiled=True)  30.5 us
  transfers between devices with their start and end apart: 8, of which 6 were waited for; matrix products, arithmetic and copies ran while one was open for 0% of the time, Pallas kernels for 0%

commit v1 on v0

--- a/solution.py
+++ b/solution.py
@@ -2,6 +2,13 @@
 import jax.numpy as jnp
 from jax import lax
 from jax.sharding import PartitionSpec as P
+
+
+def exchange_gather(block, mesh_axis, dim):
+    count = lax.axis_size(mesh_axis)
+    blocks = jnp.stack([block for _ in range(count)])
+    blocks = lax.all_to_all(blocks, mesh_axis, split_axis=0, concat_axis=0)
+    return jnp.concatenate(blocks, axis=dim)
 
 
 def with_halo(block, sides, width, periodic):
@@ -60,7 +67,7 @@
     hidden = jax.nn.gelu(pre, approximate=False).astype(jnp.bfloat16)
     partial_out = lax.dot_general(
         hidden,
-        lax.all_gather(down_weight, "lon", axis=0, tiled=True),
+        exchange_gather(down_weight, "lon", 0),
         (((1,), (1,)), ((), ())),
         preferred_element_type=jnp.float32,
     )

time: 1330 us -> 762 us (0.57)
  waiting for transfers between devices: 1260 us -> 678 us
    all_gather x1 -> x0, waiting for transfers between devices: 582 us -> none  [local(): lax.all_gather(down_weight, 'lon', axis=0, tiled=True)]
  transfers between devices with their start and end apart: 8 -> 8, of which waited for: 6 -> 4; matrix products, arithmetic and copies ran while one was open for 0% -> 2% of each run, Pallas kernels for 0% -> 0%
where the time goes in v1:
time: 762 us; the launch traced here: 761 us
  waiting for transfers between devices  678 us (89%)
  starting transfers between devices  36.3 us (5%)
  matrix products  15.5 us (2%)
  other arithmetic  13.5 us (2%)
  between operations  13.3 us (2%)
    all_gather x1, waiting for transfers between devices, local(): lax.all_gather(up_weight, 'lon', axis=0, tiled=True)  505 us
    reduce_scatter x1, waiting for transfers between devices, local(): lax.psum_scatter(partial_out.astype(jnp.bfloat16), 'lat', scatter_dimensi...  131 us
    all_gather x1, waiting for transfers between devices, local(): gathered = lax.all_gather(normed, 'lat', axis=0, tiled=True)  35.2 us
    dot_general x1, matrix products, local(): lax.dot_general(hidden, exchange_gather(down_weight, 'lon', 0), (((1,), (...  15.5 us
  transfers between devices with their start and end apart: 8, of which 4 were waited for; matrix products, arithmetic and copies ran while one was open for 2% of the time, Pallas kernels for 0%

profile of v1, /device:TPU:1, one launch (start us, length us, event | category | flops | bytes accessed | tf_op | source)
XLA Modules:
  0.0 761.1 jit_solution(5168302659967119073)
XLA Ops:
  6.5 2.1 fusion.112
  8.7 4.0 collective-permute-start
  12.7 13.0 %collective-permute-start.1 = (bf16[32,3,1024]{2,1,0:T(4,128)(2,1)S(1)}, bf16[32,3,1024]{2,1,0:T(4,128)(2,1)S(1)}, u32[]{:S(2)}, u32[]{:S(2)}) collective-permute-start(bf16[32,3,1024]{2,1,0:T(4,128)(2,1)S(1)} %get-tuple-element.12), channel_id=1, source_target_pairs={{1,0},{2,1},{3,2},{4,3},{5,4},{6,5},{7,6},{8,7},{9,8},{10,9},{11,1... | collective-permute-start | bytes 589832 | tf_op jit(solution)/shard_map/ppermute | solution.py:24
  25.8 2.3 stack.2
  28.1 0.0 copy-start.1
  28.1 0.0 copy-start
  28.1 10.8 %all-to-all-start = ((bf16[128,8,1024]{2,1,0:T(8,128)(2,1)}), bf16[128,8,1024]{2,1,0:T(8,128)(2,1)S(1)}, u32[]{:S(2)}, u32[]{:S(2)}) async-start(bf16[128,8,1024]{2,1,0:T(8,128)(2,1)} %stack.2), calls=%async_computation | async-start | bytes 4194304 | tf_op jit(solution)/shard_map/all_to_all | solution.py:10
  38.9 0.0 all-gather.3.cloned.1.call-start
  38.9 0.0 copy-done.1
  38.9 0.1 fusion.113
  39.0 0.1 fusion.114
  39.1 0.0 copy-done
  39.2 0.0 collective-permute-done
  39.2 0.0 collective-permute-done.1
  39.2 0.1 pad_maximum_fusion.4
  39.3 6.2 collective-permute-start.2
  45.5 0.0 copy-start.2
  45.5 1.9 collective-permute-start.3
  47.5 0.2 constant_dynamic-update-slice_fusion
  47.6 0.0 collective-permute-done.2
  47.7 5.7 collective-permute-done.3
  53.3 0.6 maximum_maximum_fusion
  54.0 0.0 copy-done.2
  54.0 0.0 copy-start.3
  54.0 0.0 copy-start.4
  54.0 9.4 %fusion.110 = (f32[32,8]{1,0:T(8,128)S(1)}, f32[32,8,1024]{2,1,0:T(8,128)S(1)}) fusion(f32[1024]{0:T(1024)S(1)} %bitcast.109, bf16[35,14,1024]{2,1,0:T(8,128)(2,1)S(1)} %get-tuple-element.8, f32[1024]{0:T(1024)S(1)} %bitcast.108, f32[1024]{0:T(1024)S(1)} %bitcast.107, f32[1024]{0:T(1024)S(1)} %bitcast.106, f32[1024]{0:T(1024)S(1)} %bitcast.105, ...), kind=kLoop, calls=%fused_computation.132 | loop fusion | flops 41156352 | bytes 25568256 | tf_op jit(solution)/shard_map/reduce_sum | solution.py:52
  63.5 0.0 copy-start.7
  63.5 0.3 multiply_reduce_fusion
  63.7 0.0 copy-done.3
  63.7 0.0 copy-done.4
  63.8 1.0 fusion.77
  64.8 0.0 all-gather.3.cloned.1.call-update
  64.8 0.0 all-gather.5.cloned.1.call-start
  64.9 0.7 all-gather.5.cloned.1.call-update
  65.6 0.2 reduce-scatter.2.cloned.1.call-start
  65.8 35.2 %all-gather.3.cloned.1.call-done = bf16[1024,1024]{1,0:T(8,128)(2,1)} async-done(((bf16[256,1024]{1,0:T(8,128)(2,1)}), bf16[1024,1024]{1,0:T(8,128)(2,1)}) %all-gather.3.cloned.1.call-update) | async-done | bytes 2097168 | tf_op jit(solution)/shard_map/all_gather | solution.py:58
  101.0 505.3 %all-gather.5.cloned.1.call-done = bf16[1024,1024]{1,0:T(8,128)(2,1)} async-done(((bf16[8,1024]{1,0:T(8,128)(2,1)}), bf16[1024,1024]{1,0:T(8,128)(2,1)}) %all-gather.5.cloned.1.call-update) | async-done | bytes 2097168 | tf_op jit(solution)/shard_map/all_gather | solution.py:62
  606.3 0.0 all-to-all-done
  606.3 0.0 copy-done.7
  606.3 15.5 %fusion.45 = bf16[1024,1024]{1,0:T(8,128)(2,1)} fusion(bf16[128,8,1024]{2,1,0:T(8,128)(2,1)S(1)} %all-to-all-done, f32[1024]{0:T(1024)S(1)} %copy-done.7, bf16[1024,1024]{1,0:T(8,128)(2,1)} %all-gather.3.cloned.1.call-done, bf16[1024,1024]{1,0:T(8,128)(2,1)} %all-gather.5.cloned.1.call-done), kind=kOutput, calls=%fused_computation.52 | convolution fusion | flops 4365221888 | bytes 8392704 | tf_op jit(solution)/shard_map/dot_general | solution.py:68
  621.9 0.0 copy-start.5
  621.9 0.0 copy-start.6
  621.9 0.0 reduce-scatter.2.cloned.1.call-update
  621.9 130.6 %reduce-scatter.2.cloned.1.call-done = bf16[256,1024]{1,0:T(8,128)(2,1)} async-done(((bf16[1024,1024]{1,0:T(8,128)(2,1)}), bf16[256,1024]{1,0:T(8,128)(2,1)}) %reduce-scatter.2.cloned.1.call-update) | async-done | bytes 524304 | tf_op jit(solution)/shard_map/reduce_scatter | solution.py:74
  752.5 0.0 copy-done.5
  752.5 0.0 copy-done.6
  752.5 2.0 fusion.75
  (4 shorter events, 0.1 us)
Async XLA Ops:
  8.7 30.5 %collective-permute-start = (bf16[32,3,1024]{2,1,0:T(4,128)(2,1)}, bf16[32,3,1024]{2,1,0:T(4,128)(2,1)S(1)}, u32[]{:S(2)}, u32[]{:S(2)}) collective-permute-start(bf16[32,3,1024]{2,1,0:T(4,128)(2,1)} %get-tuple-element.11), channel_id=1, source_target_pairs={{0,1},{1,2},{2,3},{3,4},{4,5},{5,6},{6,7},{7,8},{8,9},{9,10},{10,1... | collective-permute-start | bytes 589832 | tf_op jit(solution)/shard_map/ppermute | solution.py:21
  12.7 26.5 %collective-permute-start.1 = (bf16[32,3,1024]{2,1,0:T(4,128)(2,1)S(1)}, bf16[32,3,1024]{2,1,0:T(4,128)(2,1)S(1)}, u32[]{:S(2)}, u32[]{:S(2)}) collective-permute-start(bf16[32,3,1024]{2,1,0:T(4,128)(2,1)S(1)} %get-tuple-element.12), channel_id=1, source_target_pairs={{1,0},{2,1},{3,2},{4,3},{5,4},{6,5},{7,6},{8,7},{9,8},{10,9},{11,1... | collective-permute-start | bytes 589832 | tf_op jit(solution)/shard_map/ppermute | solution.py:24
  28.1 10.8 %copy-start.1 = (bf16[7,7,1024]{2,1,0:T(8,128)(2,1)S(1)}, bf16[7,7,1024]{2,1,0:T(8,128)(2,1)}, u32[]{:S(2)}) copy-start(bf16[7,7,1024]{2,1,0:T(8,128)(2,1)} %param.11) | copy-start | bytes 301060
  28.1 11.0 %copy-start = (bf16[32,8,1024]{2,1,0:T(8,128)(2,1)S(1)}, bf16[32,8,1024]{2,1,0:T(8,128)(2,1)}, u32[]{:S(2)}) copy-start(bf16[32,8,1024]{2,1,0:T(8,128)(2,1)} %param.10) | copy-start | bytes 1572868
  28.1 578.2 %all-to-all-start = ((bf16[128,8,1024]{2,1,0:T(8,128)(2,1)}), bf16[128,8,1024]{2,1,0:T(8,128)(2,1)S(1)}, u32[]{:S(2)}, u32[]{:S(2)}) async-start(bf16[128,8,1024]{2,1,0:T(8,128)(2,1)} %stack.2), calls=%async_computation | async-start | bytes 4194304 | tf_op jit(solution)/shard_map/all_to_all | solution.py:10
  38.9 62.2 %all-gather.3.cloned.1.call-start = ((), (), s32[]{:S(2)}) async-start(), calls=%async_computation.2 | async-start | bytes 2621440 | tf_op jit(solution)/shard_map/all_gather | solution.py:58
  39.3 8.4 %collective-permute-start.2 = (bf16[3,14,1024]{2,1,0:T(8,128)(2,1)S(1)}, bf16[3,14,1024]{2,1,0:T(8,128)(2,1)S(1)}, u32[]{:S(2)}, u32[]{:S(2)}) collective-permute-start(bf16[3,14,1024]{2,1,0:T(8,128)(2,1)S(1)} %get-tuple-element.9), channel_id=1, source_target_pairs={{0,128},{128,256},{256,384},{1,129},{129,257},{257,385},{2,130},{1... | collective-permute-start | bytes 258056 | tf_op jit(solution)/shard_map/ppermute | solution.py:21
  45.5 8.5 %copy-start.2 = (f32[1024]{0:T(1024)S(1)}, f32[1024]{0:T(1024)}, u32[]{:S(2)}) copy-start(f32[1024]{0:T(1024)} %param.12) | copy-start | bytes 12292
  45.5 7.8 %collective-permute-start.3 = (bf16[3,14,1024]{2,1,0:T(8,128)(2,1)S(1)}, bf16[3,14,1024]{2,1,0:T(8,128)(2,1)S(1)}, u32[]{:S(2)}, u32[]{:S(2)}) collective-permute-start(bf16[3,14,1024]{2,1,0:T(8,128)(2,1)S(1)} %get-tuple-element.10), channel_id=1, source_target_pairs={{128,0},{256,128},{384,256},{129,1},{257,129},{385,257},{130,2},{2... | collective-permute-start | bytes 258056 | tf_op jit(solution)/shard_map/ppermute | solution.py:24
  54.0 9.7 %copy-start.3 = (f32[1024]{0:T(1024)S(1)}, f32[1024]{0:T(1024)}, u32[]{:S(2)}) copy-start(f32[1024]{0:T(1024)} %param.14) | copy-start | bytes 12292
  54.0 9.7 %copy-start.4 = (f32[1024]{0:T(1024)S(1)}, f32[1024]{0:T(1024)}, u32[]{:S(2)}) copy-start(f32[1024]{0:T(1024)} %param.13) | copy-start | bytes 12292
  63.5 542.9 %copy-start.7 = (f32[1024]{0:T(1024)S(1)}, f32[1024]{0:T(1024)}, u32[]{:S(2)}) copy-start(f32[1024]{0:T(1024)} %param.16) | copy-start | bytes 12292
  64.8 541.5 %all-gather.5.cloned.1.call-start = ((), (), s32[]{:S(2)}) async-start(), calls=%async_computation.3 | async-start | bytes 2113536 | tf_op jit(solution)/shard_map/all_gather | solution.py:62
  65.6 686.9 %reduce-scatter.2.cloned.1.call-start = ((), (), s32[]{:S(2)}) async-start(), calls=%async_computation.4 | async-start | bytes 2621440 | tf_op jit(solution)/shard_map/reduce_scatter | solution.py:74
  621.9 130.6 %copy-start.5 = (f32[1024]{0:T(1024)S(1)}, f32[1024]{0:T(1024)}, u32[]{:S(2)}) copy-start(f32[1024]{0:T(1024)} %param.18) | copy-start | bytes 12292
  621.9 130.6 %copy-start.6 = (f32[1024]{0:T(1024)S(1)}, f32[1024]{0:T(1024)}, u32[]{:S(2)}) copy-start(f32[1024]{0:T(1024)} %param.19) | copy-start | bytes 12292
Sparse Core Ops, SparseCore 0:
  64.9 36.0 all-gather.2
  103.1 503.1 all-gather.4
  622.0 130.4 reduce-scatter.1
